TPU v7x, 256 devices: a whole 4x4x8 slice. The times are simulated.
256 devices in a mesh: section: 8 (over y, x_hi), ctx: 32 (over x_lo, z, core).
Axes of the slice: x: 4 (x_hi: 2, x_lo: 2; x = x_hi * 2 + x_lo), y: 4, z: 8, core: 2. Of those that a mesh axis runs over, the one named last changes fastest.
Arguments:
- queries: bfloat16 [8, 12288, 40, 128], P('section', 'ctx'), may hold values from -60 to 60
- keys_values: bfloat16 [12288, 2, 40, 128], P('ctx', None, 'section'), may hold values from -6 to 6
- positions: int32 [12288], P('ctx'), may hold values from 0 to 1533, as said below
- documents: int32 [12288], P('ctx'), may hold values from 0 to 12287, as said below
Outputs:
- attended: bfloat16 [8, 12288, 40, 128], P('section', 'ctx')
Inputs may be any that keep to these rules, and one draw needn't show every extreme that they name: `documents`: Non-decreasing along the sequence; each document is a run of 1 to 384 tokens sharing one id, one document has exactly 384 tokens, and the last document's id is 12287. `positions`: within a document the ids rise by 1 to 3 from each token to the next; a document's first id is 0 to 384.
All inputs are finite; a program needn't handle non-finite values.
Results may differ from a plain program's by a relative error of at most 0.01.
Values may be sent and summed in bfloat16 or wider, within the bound.
A program may use at most 128 MiB of HBM per device.

v0:
```python
import jax
import jax.numpy as jnp
from jax import lax
from jax.sharding import PartitionSpec as P


def shifted(block, axis, distance):
    devices = range(lax.axis_size(axis))
    route = [(i - distance, i) for i in devices if i - distance in devices]
    return lax.ppermute(block, axis, route)


def rotate(values, token_positions):
    half_dim = values.shape[-1] // 2
    exponent = jnp.arange(half_dim, dtype=jnp.float32) * (2.0 / values.shape[-1])
    inverse = jnp.power(jnp.float32(10000.0), -exponent)
    angles = token_positions.astype(jnp.float32)[:, None] * inverse[None, :]
    cosine = jnp.cos(angles)[:, None, :]
    sine = jnp.sin(angles)[:, None, :]
    widened = values.astype(jnp.float32)
    lower = widened[..., :half_dim]
    upper = widened[..., half_dim:]
    joined = jnp.concatenate(
        [lower * cosine - upper * sine, upper * cosine + lower * sine], axis=-1
    )
    return joined.astype(jnp.bfloat16)


def attend(rotated, piece, key_docs, query_docs):
    query_rows = query_docs.shape[0]
    key_rows = key_docs.shape[0]
    head_count = piece.shape[2]
    head_dim = piece.shape[3]
    factor = max((option for option in range(1, 9) if head_count % option == 0))
    groups = head_count // factor

    def split_heads(values, length):
        return jnp.moveaxis(values.reshape(length, groups, factor, head_dim), 1, 0)

    allowed = jnp.logical_and(
        key_docs[None, :] == query_docs[:, None],
        jnp.arange(key_rows)[None, :] <= jnp.arange(query_rows)[:, None] + (key_rows - query_rows),
    )
    scale = head_dim ** (-0.5)

    def one_group(operands):
        query_part, key_part, value_part = operands
        scores = (
            jnp.einsum("qhd,khd->hqk", query_part, key_part, preferred_element_type=jnp.float32)
            * scale
        )
        scores = jnp.where(allowed[None], scores, -1e30)
        largest = jnp.max(scores, axis=-1, keepdims=True)
        weights = jnp.exp(scores - largest)
        probs = (weights / jnp.sum(weights, axis=-1, keepdims=True)).astype(jnp.bfloat16)
        mixed = jnp.einsum("hqk,khd->qhd", probs, value_part, preferred_element_type=jnp.float32)
        return mixed.astype(jnp.bfloat16)

    output = lax.map(
        one_group,
        (
            split_heads(rotated, query_rows),
            split_heads(piece[:, 0], key_rows),
            split_heads(piece[:, 1], key_rows),
        ),
    )
    return jnp.moveaxis(output, 0, 1).reshape(query_rows, head_count, head_dim)


def body(queries, keys_values, positions, documents):
    rotated = rotate(queries[0], positions)
    key_share = rotate(keys_values[:, 0], positions)
    share = jnp.stack([key_share, keys_values[:, 1]], axis=1)
    at_start = lax.axis_index("ctx") == 0
    whole = lax.all_gather(share, "section", axis=2, tiled=True)
    earlier, earlier_docs = shifted((whole, documents), "ctx", 1)
    key_docs = jnp.concatenate(
        [jnp.where(at_start, -1, earlier_docs).astype(jnp.int32), documents], axis=0
    )
    window = jnp.concatenate([earlier, whole], axis=0)
    result = attend(rotated, window, key_docs, documents)
    return result[None]


def solution(mesh):
    placed = (P("section", "ctx", None, None), P("ctx", None, "section", None), P("ctx"), P("ctx"))
    return jax.shard_map(
        body, mesh=mesh, in_specs=placed, out_specs=P("section", "ctx", None, None), check_vma=False
    )
```

profile of v0, /device:TPU:2, one launch (start us, length us, event | category | flops | bytes accessed | tf_op | source)
XLA Modules:
  0.0 344.2 jit_solution(13861718311189007667)
XLA Ops:
  6.5 0.7 convert_element_type.37
  7.2 3.3 fusion.33
  10.5 0.7 copy.20
  11.2 0.1 bitcast_convert_fusion.1
  11.3 0.7 copy.21
  12.0 0.4 multiply_cosine_fusion
  12.4 0.1 fusion.29
  12.5 1.1 pad_maximum_fusion
  13.6 0.0 all-gather.2.cloned.1.call-update
  13.6 109.1 %all-gather.2.cloned.1.call-done = bf16[384,2,40,128]{0,3,2,1:T(8,128)(2,1)} async-done(((bf16[384,2,5,128]{0,3,2,1:T(8,128)(2,1)}), bf16[384,2,40,128]{0,3,2,1:T(8,128)(2,1)}) %all-gather.2.cloned.1.call-update) | async-done | bytes 7864336 | tf_op jit(solution)/shard_map/all_gather | solution.py:75
  122.7 1.9 collective-permute-start
  124.6 3.6 %collective-permute-start.1 = (s32[384]{0:T(512)S(1)}, s32[384]{0:T(512)S(1)}, u32[]{:S(2)}, u32[]{:S(2)}) collective-permute-start(s32[384]{0:T(512)S(1)} %copy-done), channel_id=1, source_target_pairs={{0,1},{1,2},{2,3},{3,4},{4,5},{5,6},{6,7},{7,8},{8,9},{9,10},{10,1... | collective-permute-start | bytes 4616 | tf_op jit(solution)/shard_map/ppermute | solution.py:10
  128.2 0.1 copy.14
  128.3 0.1 copy.15
  128.4 2.6 bitcast_convert_fusion
  131.1 2.6 subtract_convert_fusion
  133.7 0.9 copy.16
  134.7 0.9 copy.17
  135.6 4.1 %maximum_bitcast_fusion = bf16[5,384,8,128]{3,1,2,0:T(8,128)(2,1)} fusion(bf16[384,5,8,64]{3,0,2,1:T(8,128)(2,1)S(1)} %bitcast.53, bf16[384,5,8,64]{3,0,2,1:T(8,128)(2,1)S(1)} %bitcast.52), kind=kLoop, calls=%fused_computation.28 | loop fusion | flops 7864320 | bytes 7864320 | tf_op jit(solution)/shard_map/transpose | solution.py:38
  139.7 74.6 %collective-permute-done.1 = s32[384]{0:T(512)S(1)} collective-permute-done((s32[384]{0:T(512)S(1)}, s32[384]{0:T(512)S(1)}, u32[]{:S(2)}, u32[]{:S(2)}) %collective-permute-start.1) | collective-permute-done | bytes 1568 | tf_op jit(solution)/shard_map/ppermute | solution.py:10
  214.3 0.0 slice-start.1
  214.3 0.0 collective-permute-done
  214.3 8.1 %constant_dynamic-update-slice_fusion.1 = bf16[768,2,40,128]{0,3,2,1:T(8,128)(2,1)} fusion(bf16[384,2,40,128]{0,3,2,1:T(8,128)(2,1)} %collective-permute-done), kind=kLoop, calls=%fused_computation.39 | loop fusion | bytes 15728640
  222.4 4.3 %constant_dynamic-update-slice_fusion = bf16[768,2,40,128]{0,3,2,1:T(8,128)(2,1)} fusion(bf16[768,2,40,128]{0,3,2,1:T(8,128)(2,1)} %constant_dynamic-update-slice_fusion.1, bf16[384,2,40,128]{0,3,2,1:T(8,128)(2,1)S(1)} %bitcast.55), kind=kLoop, calls=%fused_computation.38 | loop fusion | bytes 15728640 | tf_op jit(solution)/shard_map/concatenate | solution.py:80
  226.7 11.1 %fusion.32 = (bf16[768,1,40,128]{0,3,2,1:T(8,128)(2,1)}, bf16[768,1,40,128]{0,3,2,1:T(8,128)(2,1)}) fusion(bf16[768,2,40,128]{0,3,2,1:T(8,128)(2,1)} %constant_dynamic-update-slice_fusion), kind=kLoop, calls=%fused_computation.45 | loop fusion | bytes 31457280 | tf_op jit(solution)/shard_map/slice | solution.py:63
  237.8 10.6 %copy.18 = bf16[768,5,8,128]{3,0,2,1:T(8,128)(2,1)} copy(bf16[768,5,8,128]{0,3,2,1:T(8,128)(2,1)} %bitcast.51) | data formatting | bytes 15728640 | tf_op jit(solution)/shard_map/reshape;squeeze | solution.py:38
  248.4 82.5 %while.11 = (s32[]{:T(128)}, bf16[5,384,8,128]{1,3,2,0:T(8,128)(2,1)}, bf16[5,768,8,128]{1,3,2,0:T(8,128)(2,1)}, bf16[5,384,8,128]{3,1,2,0:T(8,128)(2,1)}, bf16[...) while((s32[]{:T(128)}, ...), condition=%wide.region_3.4_spmd.clone, body=%wide.region_0.3_spmd.clone.sunk | while | flops 1228112640 | bytes 43090012 | solution.py:59
  248.4 3.0 fusion.44
  251.5 0.4 fusion.45
  251.9 6.5 %fusion.46 = (f32[8,384]{1,0:T(8,128)S(1)}, f32[8,384,768]{2,1,0:T(8,128)}) fusion(f32[8,384,768]{2,1,0:T(8,128)S(1)} %fusion.44, pred[384,768]{1,0:T(8,128)(4,1)S(1)} %fusion.45), kind=kOutput, calls=%fused_computation.44.clone.1 | output fusion | flops 14156543 | bytes 19181568 | tf_op jit(solution)/shard_map/while/body/eval_jaxpr/sub | solution.py:54
  258.3 6.6 %fusion.47 = bf16[5,384,8,128]{1,3,2,0:T(8,128)(2,1)} fusion(bf16[5,384,8,128]{1,3,2,0:T(8,128)(2,1)} %get-tuple-element.150, s32[]{:T(128)} %get-tuple-element.149, f32[8,384,768]{2,1,0:T(8,128)} %get-tuple-element.138, f32[8,384]{1,0:T(8,128)S(1)} %get-tuple-element.139, bf16[5,768,8,128]{1,3,2,0:T(8,128)(2,1)} %get-tuple-element.160), kind=kOutput, calls=%fused_computation.17.clone.1 | convolution fusion | flops 609091584 | bytes 11809792 | tf_op jit(solution)/shard_map/while/body/eval_jaxpr/hqk,khd->qhd/dot_general | solution.py:56
  265.0 3.0 fusion.44
  268.0 0.4 fusion.45
  268.4 6.5 %fusion.46 = (f32[8,384]{1,0:T(8,128)S(1)}, f32[8,384,768]{2,1,0:T(8,128)}) fusion(f32[8,384,768]{2,1,0:T(8,128)S(1)} %fusion.44, pred[384,768]{1,0:T(8,128)(4,1)S(1)} %fusion.45), kind=kOutput, calls=%fused_computation.44.clone.1 | output fusion | flops 14156543 | bytes 19181568 | tf_op jit(solution)/shard_map/while/body/eval_jaxpr/sub | solution.py:54
  274.9 6.6 %fusion.47 = bf16[5,384,8,128]{1,3,2,0:T(8,128)(2,1)} fusion(bf16[5,384,8,128]{1,3,2,0:T(8,128)(2,1)} %get-tuple-element.150, s32[]{:T(128)} %get-tuple-element.149, f32[8,384,768]{2,1,0:T(8,128)} %get-tuple-element.138, f32[8,384]{1,0:T(8,128)S(1)} %get-tuple-element.139, bf16[5,768,8,128]{1,3,2,0:T(8,128)(2,1)} %get-tuple-element.160), kind=kOutput, calls=%fused_computation.17.clone.1 | convolution fusion | flops 609091584 | bytes 11809792 | tf_op jit(solution)/shard_map/while/body/eval_jaxpr/hqk,khd->qhd/dot_general | solution.py:56
  281.5 3.0 fusion.44
  284.5 0.4 fusion.45
  284.9 6.5 %fusion.46 = (f32[8,384]{1,0:T(8,128)S(1)}, f32[8,384,768]{2,1,0:T(8,128)}) fusion(f32[8,384,768]{2,1,0:T(8,128)S(1)} %fusion.44, pred[384,768]{1,0:T(8,128)(4,1)S(1)} %fusion.45), kind=kOutput, calls=%fused_computation.44.clone.1 | output fusion | flops 14156543 | bytes 19181568 | tf_op jit(solution)/shard_map/while/body/eval_jaxpr/sub | solution.py:54
  291.4 6.5 %fusion.47 = bf16[5,384,8,128]{1,3,2,0:T(8,128)(2,1)} fusion(bf16[5,384,8,128]{1,3,2,0:T(8,128)(2,1)} %get-tuple-element.150, s32[]{:T(128)} %get-tuple-element.149, f32[8,384,768]{2,1,0:T(8,128)} %get-tuple-element.138, f32[8,384]{1,0:T(8,128)S(1)} %get-tuple-element.139, bf16[5,768,8,128]{1,3,2,0:T(8,128)(2,1)} %get-tuple-element.160), kind=kOutput, calls=%fused_computation.17.clone.1 | convolution fusion | flops 609091584 | bytes 11809792 | tf_op jit(solution)/shard_map/while/body/eval_jaxpr/hqk,khd->qhd/dot_general | solution.py:56
  297.9 3.0 fusion.44
  301.0 0.4 fusion.45
  301.3 6.5 %fusion.46 = (f32[8,384]{1,0:T(8,128)S(1)}, f32[8,384,768]{2,1,0:T(8,128)}) fusion(f32[8,384,768]{2,1,0:T(8,128)S(1)} %fusion.44, pred[384,768]{1,0:T(8,128)(4,1)S(1)} %fusion.45), kind=kOutput, calls=%fused_computation.44.clone.1 | output fusion | flops 14156543 | bytes 19181568 | tf_op jit(solution)/shard_map/while/body/eval_jaxpr/sub | solution.py:54
  307.8 6.7 %fusion.47 = bf16[5,384,8,128]{1,3,2,0:T(8,128)(2,1)} fusion(bf16[5,384,8,128]{1,3,2,0:T(8,128)(2,1)} %get-tuple-element.150, s32[]{:T(128)} %get-tuple-element.149, f32[8,384,768]{2,1,0:T(8,128)} %get-tuple-element.138, f32[8,384]{1,0:T(8,128)S(1)} %get-tuple-element.139, bf16[5,768,8,128]{1,3,2,0:T(8,128)(2,1)} %get-tuple-element.160), kind=kOutput, calls=%fused_computation.17.clone.1 | convolution fusion | flops 609091584 | bytes 11809792 | tf_op jit(solution)/shard_map/while/body/eval_jaxpr/hqk,khd->qhd/dot_general | solution.py:56
  314.5 3.0 fusion.44
  317.6 0.4 fusion.45
  317.9 6.5 %fusion.46 = (f32[8,384]{1,0:T(8,128)S(1)}, f32[8,384,768]{2,1,0:T(8,128)}) fusion(f32[8,384,768]{2,1,0:T(8,128)S(1)} %fusion.44, pred[384,768]{1,0:T(8,128)(4,1)S(1)} %fusion.45), kind=kOutput, calls=%fused_computation.44.clone.1 | output fusion | flops 14156543 | bytes 19181568 | tf_op jit(solution)/shard_map/while/body/eval_jaxpr/sub | solution.py:54
  324.4 6.6 %fusion.47 = bf16[5,384,8,128]{1,3,2,0:T(8,128)(2,1)} fusion(bf16[5,384,8,128]{1,3,2,0:T(8,128)(2,1)} %get-tuple-element.150, s32[]{:T(128)} %get-tuple-element.149, f32[8,384,768]{2,1,0:T(8,128)} %get-tuple-element.138, f32[8,384]{1,0:T(8,128)S(1)} %get-tuple-element.139, bf16[5,768,8,128]{1,3,2,0:T(8,128)(2,1)} %get-tuple-element.160), kind=kOutput, calls=%fused_computation.17.clone.1 | convolution fusion | flops 609091584 | bytes 11809792 | tf_op jit(solution)/shard_map/while/body/eval_jaxpr/hqk,khd->qhd/dot_general | solution.py:56
  331.0 6.4 %copy.19 = bf16[384,5,8,128]{3,2,1,0:T(8,128)(2,1)} copy(bf16[384,5,8,128]{0,3,2,1:T(8,128)(2,1)} %bitcast.13) | data formatting | bytes 7864320 | tf_op jit(solution)/shard_map/transpose | solution.py:67
  (12 shorter events, 0.0 us)
Async XLA Ops:
  6.5 118.1 %copy-start = (s32[384]{0:T(512)S(1)}, s32[384]{0:T(512)}, u32[]{:S(2)}) copy-start(s32[384]{0:T(512)} %param.9) | copy-start | bytes 4612
  6.5 116.1 %all-gather.2.cloned.1.call-start = ((), (), s32[]{:S(2)}) async-start(), calls=%async_computation | async-start | bytes 8847360 | tf_op jit(solution)/shard_map/all_gather | solution.py:75
  122.7 91.6 %collective-permute-start = (bf16[384,2,40,128]{0,3,2,1:T(8,128)(2,1)}, bf16[384,2,40,128]{0,3,2,1:T(8,128)(2,1)}, u32[]{:S(2)}, u32[]{:S(2)}) collective-permute-start(bf16[384,2,40,128]{0,3,2,1:T(8,128)(2,1)} %all-gather.2.cloned.1.call-done), channel_id=1, source_target_pairs={{0,1},{1,2},{2,3},{3,4},{4,5},{5,6},{6,7},{7,8},{8,9},{9,10},{10,1... | collective-permute-start | bytes 23592968 | tf_op jit(solution)/shard_map/ppermute | solution.py:10
  124.6 89.6 %collective-permute-start.1 = (s32[384]{0:T(512)S(1)}, s32[384]{0:T(512)S(1)}, u32[]{:S(2)}, u32[]{:S(2)}) collective-permute-start(s32[384]{0:T(512)S(1)} %copy-done), channel_id=1, source_target_pairs={{0,1},{1,2},{2,3},{3,4},{4,5},{5,6},{6,7},{7,8},{8,9},{9,10},{10,1... | collective-permute-start | bytes 4616 | tf_op jit(solution)/shard_map/ppermute | solution.py:10
  214.2 8.1 %slice-start = ((s8[7864320]{0:T(1024)(128)(4,1)}), s8[4194304]{0:T(1024)(128)(4,1)S(1)}, s32[]{:S(2)}) async-start(s8[7864320]{0:T(1024)(128)(4,1)} %bitcast.54), calls=%async_computation.1 | async-start | bytes 8388608
  214.3 8.1 %slice-start.1 = ((s8[7864320]{0:T(1024)(128)(4,1)}), s8[3670016]{0:T(1024)(128)(4,1)S(1)}, s32[]{:S(2)}) async-start(s8[7864320]{0:T(1024)(128)(4,1)} %bitcast.54), calls=%async_computation.2 | async-start | bytes 7340032
Sparse Core Ops, SparseCore 0:
  13.7 108.9 all-gather.1
where the time goes:
time: 345 us; the launch traced here: 344 us
  waiting for transfers between devices  184 us (53%)
  matrix products  48.2 us (14%)
  local copies, waits for them, and re-layouts  47.3 us (14%)
  other arithmetic  46 us (13%)
  between operations  13.5 us (4%)
  starting transfers between devices  5.48 us (2%)
    all_gather x1, waiting for transfers between devices, body(): whole = lax.all_gather(share, 'section', axis=2, tiled=True)  109 us
    ppermute x2, waiting for transfers between devices, shifted(): return lax.ppermute(block, axis, route)  74.6 us
    dot_general x5, matrix products, one_group(): jnp.einsum('hqk,khd->qhd', probs, value_part, preferred_element_type=jnp....  33 us
    sub x5, other arithmetic, one_group(): weights = jnp.exp(scores - largest)  32.5 us
    dot_general x5, matrix products, one_group(): jnp.einsum('qhd,khd->hqk', query_part, key_part, preferred_element_type=j...  15.2 us
    slice x1, local copies, waits for them, and re-layouts, attend(): piece[:, 0]  11.1 us
    another operation x1, local copies, waits for them, and re-layouts, split_heads(): return jnp.moveaxis(values.reshape(length, groups, factor, head_dim), 1, 0)  10.6 us
    unnamed x9, local copies, waits for them, and re-layouts  9.43 us
  transfers between devices with their start and end apart: 3, of which 2 were waited for; matrix products, arithmetic and copies ran while one was open for 3% of the time, Pallas kernels for 0%

commit v1 on v0

--- a/solution.py
+++ b/solution.py
@@ -1,7 +1,21 @@
+import functools
 import jax
 import jax.numpy as jnp
 from jax import lax
 from jax.sharding import PartitionSpec as P
+
+
+def watch_patch(local_values, row_axis):
+    new = jax.lax.all_to_all(
+        jnp.stack([local_values for _ in range(jax.lax.axis_size(row_axis))], axis=0),
+        row_axis,
+        split_axis=0,
+        concat_axis=0,
+    )
+    return jnp.concatenate(new, 2)
+
+
+edit_region_all = functools.partial(watch_patch, row_axis="section")
 
 
 def shifted(block, axis, distance):
@@ -72,7 +86,7 @@
     key_share = rotate(keys_values[:, 0], positions)
     share = jnp.stack([key_share, keys_values[:, 1]], axis=1)
     at_start = lax.axis_index("ctx") == 0
-    whole = lax.all_gather(share, "section", axis=2, tiled=True)
+    whole = edit_region_all(share)
     earlier, earlier_docs = shifted((whole, documents), "ctx", 1)
     key_docs = jnp.concatenate(
         [jnp.where(at_start, -1, earlier_docs).astype(jnp.int32), documents], axis=0

time: 345 us -> 313 us (0.907)
  waiting for transfers between devices: 184 us -> 74 us
  blocking collectives: 0 us -> 97.3 us
  local copies, waits for them, and re-layouts: 47.3 us -> 30.4 us
  between operations: 13.5 us -> 0.15 us
  other arithmetic: 46 us -> 56.1 us
    all_gather x1 -> x0, waiting for transfers between devices: 109 us -> none  [body(): whole = lax.all_gather(share, 'section', axis=2, tiled=True)]
    all_to_all x0 -> x1, blocking collectives: none -> 97.3 us  [watch_patch(): jax.lax.all_to_all(jnp.stack([local_values for _ in range(jax.lax.axis_si...]
    slice x1 -> x0, local copies, waits for them, and re-layouts: 11.1 us -> none  [attend(): piece[:, 0]]
    concatenate x0 -> x1, other arithmetic: none -> 11.1 us  [body(): window = jnp.concatenate([earlier, whole], axis=0)]
    unnamed x9 -> x4, local copies, waits for them, and re-layouts: 9.43 us -> 1.34 us
    concatenate x1 -> x0, local copies, waits for them, and re-layouts: 4.32 us -> none  [body(): window = jnp.concatenate([earlier, whole], axis=0)]
    all_to_all x0 -> x1, local copies, waits for them, and re-layouts: none -> 4.11 us  [watch_patch(): jax.lax.all_to_all(jnp.stack([local_values for _ in range(jax.lax.axis_si...]
  transfers between devices with their start and end apart: 3 -> 2, of which waited for: 2 -> 1; matrix products, arithmetic and copies ran while one was open for 3% -> 4% of each run, Pallas kernels for 0% -> 0%
where the time goes in v1:
time: 313 us; the launch traced here: 312 us
  blocking collectives  97.3 us (31%)
  waiting for transfers between devices  74 us (24%)
  other arithmetic  56.1 us (18%)
  matrix products  47.9 us (15%)
  local copies, waits for them, and re-layouts  30.4 us (10%)
  starting transfers between devices  6.02 us (2%)
    all_to_all x1, blocking collectives, watch_patch(): jax.lax.all_to_all(jnp.stack([local_values for _ in range(jax.lax.axis_si...  97.3 us
    ppermute x2, waiting for transfers between devices, shifted(): return lax.ppermute(block, axis, route)  74 us
    dot_general x5, matrix products, one_group(): jnp.einsum('hqk,khd->qhd', probs, value_part, preferred_element_type=jnp....  32.7 us
    sub x5, other arithmetic, one_group(): weights = jnp.exp(scores - largest)  32.5 us
    dot_general x5, matrix products, one_group(): jnp.einsum('qhd,khd->hqk', query_part, key_part, preferred_element_type=j...  15.2 us
    concatenate x1, other arithmetic, body(): window = jnp.concatenate([earlier, whole], axis=0)  11.1 us
    another operation x1, local copies, waits for them, and re-layouts, split_heads(): return jnp.moveaxis(values.reshape(length, groups, factor, head_dim), 1, 0)  10.6 us
    transpose x1, local copies, waits for them, and re-layouts, attend(): return jnp.moveaxis(output, 0, 1).reshape(query_rows, head_count, head_dim)  6.36 us
  transfers between devices with their start and end apart: 2, of which 1 were waited for; matrix products, arithmetic and copies ran while one was open for 4% of the time, Pallas kernels for 0%

profile of v1, /device:TPU:2, one launch (start us, length us, event | category | flops | bytes accessed | tf_op | source)
XLA Modules:
  0.0 312.0 jit_solution(1934835401298501805)
XLA Ops:
  0.0 0.7 convert_element_type.37
  0.7 3.2 %fusion.33 = (bf16[384,1,5,128]{3,1,2,0:T(2,128)(2,1)S(1)}, bf16[384,1,5,128]{3,1,2,0:T(2,128)(2,1)S(1)}) fusion(bf16[384,2,5,128]{3,1,2,0:T(2,128)(2,1)} %param.7), kind=kLoop, calls=%fused_computation.47 | loop fusion | bytes 1966080 | tf_op jit(solution)/shard_map/slice | solution.py:86
  3.9 0.7 copy.40
  4.6 0.1 bitcast_convert_fusion.1
  4.7 0.7 copy.41
  5.3 0.4 multiply_cosine_fusion
  5.8 0.1 fusion.30
  5.9 0.1 pad_maximum_fusion.1
  6.0 0.7 copy.32
  6.7 1.9 stack.5
  8.6 97.3 %all_to_all.5 = bf16[8,384,2,5,128]{4,1,3,2,0:T(8,128)(2,1)S(1)} all-to-all(bf16[8,384,2,5,128]{4,1,3,2,0:T(8,128)(2,1)S(1)} %stack.5), channel_id=1, replica_groups=mesh['section'=8,'ctx'=32] {'section'}, dimensions={0} | all-to-all | bytes 15728640 | tf_op jit(solution)/shard_map/all_to_all | solution.py:9
  105.9 4.1 %copy.33 = bf16[8,384,2,5,128]{4,1,3,0,2:T(8,128)(2,1)} copy(bf16[8,384,2,5,128]{4,1,3,2,0:T(8,128)(2,1)S(1)} %all_to_all.5) | data formatting | bytes 15728640 | tf_op jit(solution)/shard_map/all_to_all | solution.py:9
  110.0 1.9 collective-permute-start
  111.9 0.0 copy-done
  111.9 4.1 %collective-permute-start.1 = (s32[384]{0:T(512)S(1)}, s32[384]{0:T(512)S(1)}, u32[]{:S(2)}, u32[]{:S(2)}) collective-permute-start(s32[384]{0:T(512)S(1)} %copy-done), channel_id=1, source_target_pairs={{0,1},{1,2},{2,3},{3,4},{4,5},{5,6},{6,7},{7,8},{8,9},{9,10},{10,1... | collective-permute-start | bytes 4616 | tf_op jit(solution)/shard_map/ppermute | solution.py:24
  116.1 0.1 copy.35
  116.2 0.1 copy.36
  116.3 2.6 bitcast_convert_fusion
  119.0 2.6 subtract_convert_fusion
  121.6 0.9 copy.37
  122.5 0.9 copy.38
  123.5 4.1 %maximum_bitcast_fusion = bf16[5,384,8,128]{3,1,2,0:T(8,128)(2,1)} fusion(bf16[384,5,8,64]{3,0,2,1:T(8,128)(2,1)S(1)} %bitcast.58, bf16[384,5,8,64]{3,0,2,1:T(8,128)(2,1)S(1)} %bitcast.57), kind=kLoop, calls=%fused_computation.32 | loop fusion | flops 7864320 | bytes 7864320 | tf_op jit(solution)/shard_map/transpose | solution.py:52
  127.6 74.0 %collective-permute-done.1 = s32[384]{0:T(512)S(1)} collective-permute-done((s32[384]{0:T(512)S(1)}, s32[384]{0:T(512)S(1)}, u32[]{:S(2)}, u32[]{:S(2)}) %collective-permute-start.1) | collective-permute-done | bytes 1568 | tf_op jit(solution)/shard_map/ppermute | solution.py:24
  201.6 0.0 collective-permute-done
  201.6 11.1 %pad_maximum_fusion = (bf16[768,1,40,128]{3,0,2,1:T(8,128)(2,1)}, bf16[768,1,40,128]{3,0,2,1:T(8,128)(2,1)}) fusion(bf16[384,2,40,128]{3,0,2,1:T(8,128)(2,1)} %bitcast.55, bf16[384,2,40,128]{3,0,2,1:T(8,128)(2,1)} %collective-permute-done), kind=kLoop, calls=%fused_computation.29 | loop fusion | flops 31457280 | bytes 31457280 | tf_op jit(solution)/shard_map/concatenate | solution.py:94
  212.7 10.6 %copy.34 = bf16[768,5,8,128]{0,3,2,1:T(8,128)(2,1)} copy(bf16[768,5,8,128]{3,0,2,1:T(8,128)(2,1)} %bitcast.56) | data formatting | bytes 15728640 | tf_op jit(solution)/shard_map/reshape;squeeze | solution.py:52
  223.3 82.3 %while.11 = (s32[]{:T(128)}, bf16[5,384,8,128]{1,3,2,0:T(8,128)(2,1)}, bf16[5,768,8,128]{1,3,2,0:T(8,128)(2,1)}, bf16[5,384,8,128]{3,1,2,0:T(8,128)(2,1)}, bf16[...) while((s32[]{:T(128)}, ...), condition=%wide.region_3.4_spmd.clone, body=%wide.region_0.3_spmd.clone.sunk | while | flops 1228112640 | bytes 43090012 | solution.py:73
  223.3 3.0 fusion.44
  226.4 0.4 fusion.45
  226.7 6.5 %fusion.46 = (f32[8,384]{1,0:T(8,128)S(1)}, f32[8,384,768]{2,1,0:T(8,128)}) fusion(f32[8,384,768]{2,1,0:T(8,128)S(1)} %fusion.44, pred[384,768]{1,0:T(8,128)(4,1)S(1)} %fusion.45), kind=kOutput, calls=%fused_computation.46.clone.1 | output fusion | flops 14156543 | bytes 19181568 | tf_op jit(solution)/shard_map/while/body/eval_jaxpr/sub | solution.py:68
  233.2 6.5 %fusion.47 = bf16[5,384,8,128]{1,3,2,0:T(8,128)(2,1)} fusion(bf16[5,384,8,128]{1,3,2,0:T(8,128)(2,1)} %get-tuple-element.150, s32[]{:T(128)} %get-tuple-element.149, f32[8,384,768]{2,1,0:T(8,128)} %get-tuple-element.138, f32[8,384]{1,0:T(8,128)S(1)} %get-tuple-element.139, bf16[5,768,8,128]{1,3,2,0:T(8,128)(2,1)} %get-tuple-element.160), kind=kOutput, calls=%fused_computation.17.clone.1 | convolution fusion | flops 609091584 | bytes 11809792 | tf_op jit(solution)/shard_map/while/body/eval_jaxpr/hqk,khd->qhd/dot_general | solution.py:70
  239.8 3.0 fusion.44
  242.8 0.4 fusion.45
  243.2 6.5 %fusion.46 = (f32[8,384]{1,0:T(8,128)S(1)}, f32[8,384,768]{2,1,0:T(8,128)}) fusion(f32[8,384,768]{2,1,0:T(8,128)S(1)} %fusion.44, pred[384,768]{1,0:T(8,128)(4,1)S(1)} %fusion.45), kind=kOutput, calls=%fused_computation.46.clone.1 | output fusion | flops 14156543 | bytes 19181568 | tf_op jit(solution)/shard_map/while/body/eval_jaxpr/sub | solution.py:68
  249.7 6.6 %fusion.47 = bf16[5,384,8,128]{1,3,2,0:T(8,128)(2,1)} fusion(bf16[5,384,8,128]{1,3,2,0:T(8,128)(2,1)} %get-tuple-element.150, s32[]{:T(128)} %get-tuple-element.149, f32[8,384,768]{2,1,0:T(8,128)} %get-tuple-element.138, f32[8,384]{1,0:T(8,128)S(1)} %get-tuple-element.139, bf16[5,768,8,128]{1,3,2,0:T(8,128)(2,1)} %get-tuple-element.160), kind=kOutput, calls=%fused_computation.17.clone.1 | convolution fusion | flops 609091584 | bytes 11809792 | tf_op jit(solution)/shard_map/while/body/eval_jaxpr/hqk,khd->qhd/dot_general | solution.py:70
  256.2 3.0 fusion.44
  259.3 0.4 fusion.45
  259.6 6.5 %fusion.46 = (f32[8,384]{1,0:T(8,128)S(1)}, f32[8,384,768]{2,1,0:T(8,128)}) fusion(f32[8,384,768]{2,1,0:T(8,128)S(1)} %fusion.44, pred[384,768]{1,0:T(8,128)(4,1)S(1)} %fusion.45), kind=kOutput, calls=%fused_computation.46.clone.1 | output fusion | flops 14156543 | bytes 19181568 | tf_op jit(solution)/shard_map/while/body/eval_jaxpr/sub | solution.py:68
  266.2 6.6 %fusion.47 = bf16[5,384,8,128]{1,3,2,0:T(8,128)(2,1)} fusion(bf16[5,384,8,128]{1,3,2,0:T(8,128)(2,1)} %get-tuple-element.150, s32[]{:T(128)} %get-tuple-element.149, f32[8,384,768]{2,1,0:T(8,128)} %get-tuple-element.138, f32[8,384]{1,0:T(8,128)S(1)} %get-tuple-element.139, bf16[5,768,8,128]{1,3,2,0:T(8,128)(2,1)} %get-tuple-element.160), kind=kOutput, calls=%fused_computation.17.clone.1 | convolution fusion | flops 609091584 | bytes 11809792 | tf_op jit(solution)/shard_map/while/body/eval_jaxpr/hqk,khd->qhd/dot_general | solution.py:70
  272.7 3.0 fusion.44
  275.8 0.4 fusion.45
  276.1 6.5 %fusion.46 = (f32[8,384]{1,0:T(8,128)S(1)}, f32[8,384,768]{2,1,0:T(8,128)}) fusion(f32[8,384,768]{2,1,0:T(8,128)S(1)} %fusion.44, pred[384,768]{1,0:T(8,128)(4,1)S(1)} %fusion.45), kind=kOutput, calls=%fused_computation.46.clone.1 | output fusion | flops 14156543 | bytes 19181568 | tf_op jit(solution)/shard_map/while/body/eval_jaxpr/sub | solution.py:68
  282.6 6.5 %fusion.47 = bf16[5,384,8,128]{1,3,2,0:T(8,128)(2,1)} fusion(bf16[5,384,8,128]{1,3,2,0:T(8,128)(2,1)} %get-tuple-element.150, s32[]{:T(128)} %get-tuple-element.149, f32[8,384,768]{2,1,0:T(8,128)} %get-tuple-element.138, f32[8,384]{1,0:T(8,128)S(1)} %get-tuple-element.139, bf16[5,768,8,128]{1,3,2,0:T(8,128)(2,1)} %get-tuple-element.160), kind=kOutput, calls=%fused_computation.17.clone.1 | convolution fusion | flops 609091584 | bytes 11809792 | tf_op jit(solution)/shard_map/while/body/eval_jaxpr/hqk,khd->qhd/dot_general | solution.py:70
  289.2 3.0 fusion.44
  292.2 0.4 fusion.45
  292.6 6.5 %fusion.46 = (f32[8,384]{1,0:T(8,128)S(1)}, f32[8,384,768]{2,1,0:T(8,128)}) fusion(f32[8,384,768]{2,1,0:T(8,128)S(1)} %fusion.44, pred[384,768]{1,0:T(8,128)(4,1)S(1)} %fusion.45), kind=kOutput, calls=%fused_computation.46.clone.1 | output fusion | flops 14156543 | bytes 19181568 | tf_op jit(solution)/shard_map/while/body/eval_jaxpr/sub | solution.py:68
  299.1 6.5 %fusion.47 = bf16[5,384,8,128]{1,3,2,0:T(8,128)(2,1)} fusion(bf16[5,384,8,128]{1,3,2,0:T(8,128)(2,1)} %get-tuple-element.150, s32[]{:T(128)} %get-tuple-element.149, f32[8,384,768]{2,1,0:T(8,128)} %get-tuple-element.138, f32[8,384]{1,0:T(8,128)S(1)} %get-tuple-element.139, bf16[5,768,8,128]{1,3,2,0:T(8,128)(2,1)} %get-tuple-element.160), kind=kOutput, calls=%fused_computation.17.clone.1 | convolution fusion | flops 609091584 | bytes 11809792 | tf_op jit(solution)/shard_map/while/body/eval_jaxpr/hqk,khd->qhd/dot_general | solution.py:70
  305.6 6.4 %copy.39 = bf16[384,5,8,128]{3,2,1,0:T(8,128)(2,1)} copy(bf16[384,5,8,128]{0,3,2,1:T(8,128)(2,1)} %bitcast.15) | data formatting | bytes 7864320 | tf_op jit(solution)/shard_map/transpose | solution.py:81
  (6 shorter events, 0.0 us)
Async XLA Ops:
  105.9 6.0 %copy-start = (s32[384]{0:T(512)S(1)}, s32[384]{0:T(512)}, u32[]{:S(2)}) copy-start(s32[384]{0:T(512)} %param.9) | copy-start | bytes 4612
  110.0 91.6 %collective-permute-start = (bf16[384,2,40,128]{3,0,2,1:T(8,128)(2,1)}, bf16[384,2,40,128]{3,0,2,1:T(8,128)(2,1)}, u32[]{:S(2)}, u32[]{:S(2)}) collective-permute-start(bf16[384,2,40,128]{3,0,2,1:T(8,128)(2,1)} %bitcast.54), channel_id=1, source_target_pairs={{0,1},{1,2},{2,3},{3,4},{4,5},{5,6},{6,7},{7,8},{8,9},{9,10},{10,1... | collective-permute-start | bytes 23592968 | tf_op jit(solution)/shard_map/ppermute | solution.py:24
  111.9 89.6 %collective-permute-start.1 = (s32[384]{0:T(512)S(1)}, s32[384]{0:T(512)S(1)}, u32[]{:S(2)}, u32[]{:S(2)}) collective-permute-start(s32[384]{0:T(512)S(1)} %copy-done), channel_id=1, source_target_pairs={{0,1},{1,2},{2,3},{3,4},{4,5},{5,6},{6,7},{7,8},{8,9},{9,10},{10,1... | collective-permute-start | bytes 4616 | tf_op jit(solution)/shard_map/ppermute | solution.py:24
